TPU v7x, 256 devices: a whole 4x4x8 slice. The times are simulated.
256 devices in a mesh: row: 16 (over x_lo, y, core), col: 16 (over x_hi, z).
Axes of the slice: x: 4 (x_hi: 2, x_lo: 2; x = x_hi * 2 + x_lo), y: 4, z: 8, core: 2. Of those that a mesh axis runs over, the one named last changes fastest.
Arguments:
- slab: float32 [32768, 8192], P('row', 'col'), may hold values from -250 to 250
- sketch_op: float32 [256, 32768], P(None, 'row'), may hold values from -0.03125 to 0.03125
- block_order: int32 [64], replicated, may hold values from 0 to 63, as said below
- pivots: int32 [2, 128], replicated, may hold values from 0 to 8191, as said below
Outputs:
- slab_out: float32 [32768, 8192], P('row', 'col')
- factor_rows: float32 [256, 8192], P(None, 'col')
- sketch_out: float32 [256, 8192], P(None, 'col')
Inputs may be any that keep to these rules, and one draw needn't show every extreme that they name: A permutation of the 64 storage blocks; panel k uses block block_order[k]. `pivots`: each row holds 128 different storage columns, none of them in the storage blocks block_order[0 .. 1].
All inputs are finite; a program needn't handle non-finite values.
Results may differ from a plain program's by a relative error of at most 0.00012.
Values sent between devices are 32-bit elements; how exact they have to be, the bound alone decides.
No kernel may reach another device: no remote copies, remote signals or barrier semaphores. Data moves between devices by JAX's collectives and lax.ppermute only.
A program may use at most 64 MiB of HBM per device.

v0:
```python
import jax
import jax.numpy as jnp
from jax import lax
from jax.sharding import PartitionSpec as P


def from_root(value, axis, source):
    kept = jnp.where(lax.axis_index(axis) == source, value, 0).astype(value.dtype)
    return lax.psum(kept, axis)


def contract_rows(left, right):
    return lax.dot_general(
        left,
        right,
        (((0,), (0,)), ((), ())),
        precision=lax.Precision.HIGHEST,
        preferred_element_type=jnp.float32,
    )


def right_solve(lower_factor, values):
    return lax.linalg.triangular_solve(
        lower_factor, values, left_side=False, lower=True, transpose_a=True
    )


def local(slab, sketch_op, block_order, pivots):
    highest = lax.Precision.HIGHEST
    local_width = slab.shape[1]
    panel_width = pivots.shape[1]
    col_place = lax.axis_index("col")
    col_base = col_place * local_width
    local_cols = col_base + jnp.arange(local_width, dtype=jnp.int32)
    partial_sketch = jnp.dot(sketch_op, slab, precision=highest, preferred_element_type=jnp.float32)
    sketch = lax.psum(partial_sketch, "row")
    finished = jnp.zeros((local_width,), dtype=bool)
    factor_parts = []
    for panel_number in range(pivots.shape[0]):
        block_start = block_order[panel_number] * panel_width
        owner_col = block_start // local_width
        block_offset = block_start - owner_col * local_width
        owns_block = col_place == owner_col
        pivot_list = pivots[panel_number]
        local_index = pivot_list - col_base
        selector = (
            jnp.arange(local_width, dtype=jnp.int32)[:, None] == local_index[None, :]
        ).astype(jnp.float32)
        targeted = jnp.sum(selector, axis=1) > 0.5
        picked = jnp.dot(slab, selector, precision=highest, preferred_element_type=jnp.float32)
        picked_sketch = jnp.dot(
            sketch, selector, precision=highest, preferred_element_type=jnp.float32
        )
        own_block = lax.dynamic_slice_in_dim(slab, block_offset, panel_width, 1)
        own_sketch = lax.dynamic_slice_in_dim(sketch, block_offset, panel_width, 1)
        panel_cols, panel_sketch = lax.psum((picked, picked_sketch), "col")
        displaced, displaced_sketch = (
            from_root(own_block, "col", owner_col),
            from_root(own_sketch, "col", owner_col),
        )
        slab = lax.dynamic_update_slice_in_dim(
            slab, jnp.where(owns_block, panel_cols, own_block), block_offset, 1
        )
        placed = lax.dot_general(
            displaced,
            selector,
            (((1,), (1,)), ((), ())),
            precision=highest,
            preferred_element_type=jnp.float32,
        )
        slab = jnp.where(targeted[None, :], placed, slab)
        placed_sketch = lax.dot_general(
            displaced_sketch,
            selector,
            (((1,), (1,)), ((), ())),
            precision=highest,
            preferred_element_type=jnp.float32,
        )
        sketch = jnp.where(targeted[None, :], placed_sketch, sketch)
        gram_matrix = lax.psum(contract_rows(panel_cols, panel_cols), "row")
        lower_factor = jnp.linalg.cholesky(gram_matrix)
        ortho_basis = right_solve(lower_factor, panel_cols)
        projected = lax.psum(contract_rows(ortho_basis, slab), "row")
        in_block = local_cols // panel_width == block_order[panel_number]
        factor_parts.append(jnp.where(finished[None, :], 0.0, projected))
        finished = finished | in_block
        update = jnp.dot(
            ortho_basis, projected, precision=highest, preferred_element_type=jnp.float32
        )
        slab = jnp.where(finished[None, :], slab, slab - update)
        sketch_basis = right_solve(lower_factor, panel_sketch)
        sketch_update = jnp.dot(
            sketch_basis, projected, precision=highest, preferred_element_type=jnp.float32
        )
        sketch = jnp.where(finished[None, :], 0.0, sketch - sketch_update)
    return (slab, jnp.concatenate(factor_parts, axis=0), sketch)


def solution(mesh):
    return jax.shard_map(
        local,
        mesh=mesh,
        in_specs=(P("row", "col"), P(None, "row"), P(), P()),
        out_specs=(P("row", "col"), P(None, "col"), P(None, "col")),
        check_vma=False,
    )
```

profile of v0, /device:TPU:1, one launch (start us, length us, event | category | flops | bytes accessed | tf_op | source)
XLA Modules:
  0.0 1056.3 jit_solution(7208083732617475073)
XLA Ops:
  7.2 2.3 copy.36
  9.6 2.0 copy-done.1
  11.6 4.5 fusion.31
  17.5 2.3 dynamic-slice_select_fusion.1
  19.7 5.2 convolution_bitcast_fusion
  24.9 118.8 %all-reduce.18.cloned.1.call-done = f32[256,512]{1,0:T(8,128)} async-done(((f32[256,512]{1,0:T(8,128)}), f32[256,512]{1,0:T(8,128)}) %all-reduce.18.cloned.1.call-update) | async-done | bytes 524304 | tf_op jit(solution)/shard_map/psum | solution.py:36
  143.7 2.1 fusion.4
  145.8 1.6 dynamic-slice_select_fusion.3
  147.6 154.5 %all-reduce.22.cloned.1.call-done = (f32[2048,128]{1,0:T(8,128)}, f32[2048,128]{1,0:T(8,128)}, f32[256,128]{1,0:T(8,128)}, f32[256,128]{1,0:T(8,128)}) async-done(((f32[2048,128]{1,0:T(8,128)}, f32[2048,128]{1,0:T(8,128)}, f32[256,128]{1,0:T(8,128)}, f32[256,128]{1,0:T(8,128)}), (f32[2048,128]{1,0:T(8,128)}, f32[2048,128]{1,0:T(8,128)}, f32[256,128]{1,0:T(8,128)}, ...) | async-done | bytes 2359312 | tf_op jit(solution)/shard_map/psum | solution.py:56
  302.0 2.4 select_dynamic-update-slice_fusion.1
  304.4 2.4 fusion.27
  307.1 6.3 convolution_select_fusion.1
  313.5 113.2 %all-reduce.10.cloned.1.call-done = f32[128,128]{0,1:T(8,128)} async-done(((f32[128,128]{0,1:T(8,128)}), f32[128,128]{0,1:T(8,128)}) %all-reduce.10.cloned.1.call-update) | async-done | bytes 65552 | tf_op jit(solution)/shard_map/psum | solution.py:80
  426.6 0.9 copy.14
  427.6 0.9 fusion.22
  428.5 11.7 %cholesky.44 = f32[128,128]{1,0:T(8,128)S(1)} custom-call(f32[128,128]{1,0:T(8,128)S(1)} %fusion.22), custom_call_target="Cholesky" | custom-call | tf_op jit(solution)/shard_map/jit(cholesky)/cholesky | solution.py:81
  440.9 0.7 fusion.15
  441.5 9.8 custom-call.10
  451.3 1.1 convolution_bitcast_fusion.2
  452.4 1.0 copy-done.5
  453.4 5.3 fusion.28
  459.0 0.7 broadcast_compare_fusion.2
  460.7 124.1 %all-reduce.12.cloned.1.call-done = f32[128,512]{1,0:T(8,128)} async-done(((f32[128,512]{1,0:T(8,128)}), f32[128,512]{1,0:T(8,128)}) %all-reduce.12.cloned.1.call-update) | async-done | bytes 262160 | tf_op jit(solution)/shard_map/psum | solution.py:83
  584.8 1.6 fusion.32
  586.3 1.6 fusion.1
  587.9 1.1 fusion.5
  589.0 5.5 subtract_select_fusion.1
  594.5 3.0 fusion.6
  597.5 0.7 dynamic-slice_select_fusion.2
  598.2 1.1 dynamic-slice_select_fusion
  599.5 154.4 %all-reduce.20.cloned.1.call-done = (f32[2048,128]{1,0:T(8,128)}, f32[2048,128]{1,0:T(8,128)}, f32[256,128]{1,0:T(8,128)}, f32[256,128]{1,0:T(8,128)}) async-done(((f32[2048,128]{1,0:T(8,128)}, f32[2048,128]{1,0:T(8,128)}, f32[256,128]{1,0:T(8,128)}, f32[256,128]{1,0:T(8,128)}), (f32[2048,128]{1,0:T(8,128)}, f32[2048,128]{1,0:T(8,128)}, f32[256,128]{1,0:T(8,128)}, ...) | async-done | bytes 2359312 | tf_op jit(solution)/shard_map/psum | solution.py:56
  753.9 2.4 select_dynamic-update-slice_fusion
  756.3 2.4 fusion.29
  759.1 6.3 convolution_select_fusion
  765.4 113.1 %all-reduce.14.cloned.1.call-done = f32[128,128]{0,1:T(8,128)} async-done(((f32[128,128]{0,1:T(8,128)}), f32[128,128]{0,1:T(8,128)}) %all-reduce.14.cloned.1.call-update) | async-done | bytes 65552 | tf_op jit(solution)/shard_map/psum | solution.py:80
  878.5 0.9 copy.16
  879.5 0.9 fusion.19
  880.4 11.7 %cholesky.55 = f32[128,128]{1,0:T(8,128)S(1)} custom-call(f32[128,128]{1,0:T(8,128)S(1)} %fusion.19), custom_call_target="Cholesky" | custom-call | tf_op jit(solution)/shard_map/jit(cholesky)/cholesky | solution.py:81
  893.4 9.8 custom-call.11
  903.2 1.1 convolution_bitcast_fusion.1
  904.3 1.0 copy-done.7
  905.3 5.4 fusion.30
  910.7 1.3 compare_or_fusion
  912.3 124.4 %all-reduce.16.cloned.1.call-done = f32[128,512]{1,0:T(8,128)} async-done(((f32[128,512]{1,0:T(8,128)}), f32[128,512]{1,0:T(8,128)}) %all-reduce.16.cloned.1.call-update) | async-done | bytes 262160 | tf_op jit(solution)/shard_map/psum | solution.py:83
  1036.7 1.9 fusion.33
  1038.6 1.3 fusion.3
  1039.9 8.2 subtract_select_fusion
  1048.1 0.8 pad_maximum_fusion
  (59 shorter events, 4.6 us)
Async XLA Ops:
  7.2 4.4 copy-start
  7.2 136.5 %all-reduce.18.cloned.1.call-start = ((), (), s32[]{:S(2)}) async-start(), calls=%async_computation.4 | async-start | bytes 1048576 | tf_op jit(solution)/shard_map/psum | solution.py:36
  9.6 2.0 copy-start.1
  11.6 4.6 copy-start.15
  11.6 8.2 copy-start.16
  16.1 286.0 %all-reduce.22.cloned.1.call-start = ((), (), s32[]{:S(2)}) async-start(), calls=%async_computation.6 | async-start | bytes 4718592 | tf_op jit(solution)/shard_map/psum | solution.py:56
  147.4 279.2 %all-reduce.10.cloned.1.call-start = ((), (), s32[]{:S(2)}) async-start(), calls=%async_computation | async-start | bytes 131072 | tf_op jit(solution)/shard_map/psum | solution.py:80
  302.0 2.4 copy-start.3
  306.9 277.8 %all-reduce.12.cloned.1.call-start = ((), (), s32[]{:S(2)}) async-start(), calls=%async_computation.1 | async-start | bytes 524288 | tf_op jit(solution)/shard_map/psum | solution.py:83
  427.6 32.8 %copy-start.12 = (f32[256,128]{1,0:T(8,128)S(1)}, f32[256,128]{1,0:T(8,128)}, u32[]{:S(2)}) copy-start(f32[256,128]{1,0:T(8,128)} %get-tuple-element.12) | copy-start | bytes 393220
  452.4 1.0 copy-start.5
  458.7 130.3 %copy-start.6 = (f32[2048,128]{0,1:T(8,128)S(1)}, f32[2048,128]{0,1:T(8,128)}, u32[]{:S(2)}) copy-start(f32[2048,128]{0,1:T(8,128)} %copy-done.5) | copy-start | bytes 3145732
  458.8 295.2 %all-reduce.20.cloned.1.call-start = ((), (), s32[]{:S(2)}) async-start(), calls=%async_computation.5 | async-start | bytes 4718592 | tf_op jit(solution)/shard_map/psum | solution.py:56
  587.9 9.6 copy-start.8
  594.5 3.7 copy-start.2
  599.3 279.2 %all-reduce.14.cloned.1.call-start = ((), (), s32[]{:S(2)}) async-start(), calls=%async_computation.2 | async-start | bytes 131072 | tf_op jit(solution)/shard_map/psum | solution.py:80
  753.9 2.4 copy-start.4
  758.8 277.9 %all-reduce.16.cloned.1.call-start = ((), (), s32[]{:S(2)}) async-start(), calls=%async_computation.3 | async-start | bytes 524288 | tf_op jit(solution)/shard_map/psum | solution.py:83
  879.5 32.5 %copy-start.13 = (f32[256,128]{1,0:T(8,128)S(1)}, f32[256,128]{1,0:T(8,128)}, u32[]{:S(2)}) copy-start(f32[256,128]{1,0:T(8,128)} %get-tuple-element.8) | copy-start | bytes 393220
  903.2 135.4 %copy-start.14 = (f32[256,128]{1,0:T(8,128)S(1)}, f32[256,128]{1,0:T(8,128)}, u32[]{:S(2)}) copy-start(f32[256,128]{1,0:T(8,128)} %get-tuple-element.9) | copy-start | bytes 393220
  904.3 1.0 copy-start.7
  905.3 133.3 %copy-start.9 = (f32[256,512]{1,0:T(8,128)S(1)}, f32[256,512]{1,0:T(8,128)}, u32[]{:S(2)}) copy-start(f32[256,512]{1,0:T(8,128)} %copy-done.8) | copy-start | bytes 1572868
  1039.9 8.2 copy-start.10
  1039.9 8.2 copy-start.11
Sparse Core Ops, SparseCore 0:
  16.2 127.4 all-reduce.17
  147.5 154.4 all-reduce.21
  307.0 119.5 all-reduce.9
  458.9 125.8 all-reduce.11
  599.4 154.4 all-reduce.19
  758.9 119.5 all-reduce.13
  910.8 125.8 all-reduce.15
where the time goes:
time: 1060 us
  waiting for transfers between devices  902 us (85%)
  matrix products  66.9 us (6%)
  other arithmetic  61 us (6%)
  between operations  16.2 us (2%)
    psum x2, waiting for transfers between devices, local(): panel_cols, panel_sketch = lax.psum((picked, picked_sketch), 'col')  309 us
    psum x2, waiting for transfers between devices, local(): projected = lax.psum(contract_rows(ortho_basis, slab), 'row')  248 us
    psum x2, waiting for transfers between devices, local(): gram_matrix = lax.psum(contract_rows(panel_cols, panel_cols), 'row')  226 us
    psum x1, waiting for transfers between devices, local(): sketch = lax.psum(partial_sketch, 'row')  119 us
    another operation x6, other arithmetic, local(): lower_factor = jnp.linalg.cholesky(gram_matrix)  24.8 us
  transfers between devices with their start and end apart: 7, of which 7 were waited for; matrix products, arithmetic and copies ran while one was open for 2% of the time, Pallas kernels for 0%

commit v1 on v0

--- a/solution.py
+++ b/solution.py
@@ -2,6 +2,10 @@
 import jax.numpy as jnp
 from jax import lax
 from jax.sharding import PartitionSpec as P
+
+
+def region_direct(panel):
+    return jnp.sum(jax.lax.all_gather(panel, "row"), axis=0)
 
 
 def from_root(value, axis, source):
@@ -80,7 +84,7 @@
         gram_matrix = lax.psum(contract_rows(panel_cols, panel_cols), "row")
         lower_factor = jnp.linalg.cholesky(gram_matrix)
         ortho_basis = right_solve(lower_factor, panel_cols)
-        projected = lax.psum(contract_rows(ortho_basis, slab), "row")
+        projected = region_direct(contract_rows(ortho_basis, slab))
         in_block = local_cols // panel_width == block_order[panel_number]
         factor_parts.append(jnp.where(finished[None, :], 0.0, projected))
         finished = finished | in_block

time: 1060 us -> 897 us (0.85)
  waiting for transfers between devices: 902 us -> 735 us
    psum x2 -> x0, waiting for transfers between devices: 248 us -> none  [local(): projected = lax.psum(contract_rows(ortho_basis, slab), 'row')]
    all_gather x0 -> x2, waiting for transfers between devices: none -> 83.3 us  [region_direct(): return jnp.sum(jax.lax.all_gather(panel, 'row'), axis=0)]
  transfers between devices with their start and end apart: 7 -> 7, of which waited for: 7 -> 7; matrix products, arithmetic and copies ran while one was open for 2% -> 3% of each run, Pallas kernels for 0% -> 0%
where the time goes in v1:
time: 897 us; the launch traced here: 890 us
  waiting for transfers between devices  735 us (82%)
  other arithmetic  66.6 us (7%)
  matrix products  62.1 us (7%)
  between operations  16.2 us (2%)
    psum x2, waiting for transfers between devices, local(): panel_cols, panel_sketch = lax.psum((picked, picked_sketch), 'col')  307 us
    psum x2, waiting for transfers between devices, local(): gram_matrix = lax.psum(contract_rows(panel_cols, panel_cols), 'row')  226 us
    psum x1, waiting for transfers between devices, local(): sketch = lax.psum(partial_sketch, 'row')  119 us
    all_gather x2, waiting for transfers between devices, region_direct(): return jnp.sum(jax.lax.all_gather(panel, 'row'), axis=0)  83.3 us
    another operation x6, other arithmetic, local(): lower_factor = jnp.linalg.cholesky(gram_matrix)  24.8 us
    another operation x4, other arithmetic, right_solve(): lax.linalg.triangular_solve(lower_factor, values, left_side=False, lower=...  20.9 us
  transfers between devices with their start and end apart: 7, of which 7 were waited for; matrix products, arithmetic and copies ran while one was open for 3% of the time, Pallas kernels for 0%

profile of v1, /device:TPU:1, one launch (start us, length us, event | category | flops | bytes accessed | tf_op | source)
XLA Modules:
  0.0 889.8 jit_solution(7334969142407811742)
XLA Ops:
  7.2 2.3 copy.34
  9.6 2.0 copy-done.1
  11.6 4.5 fusion.31
  17.5 2.3 dynamic-slice_select_fusion.1
  19.8 5.2 convolution_bitcast_fusion
  24.9 118.8 %all-reduce.12.cloned.1.call-done = f32[256,512]{1,0:T(8,128)} async-done(((f32[256,512]{1,0:T(8,128)}), f32[256,512]{1,0:T(8,128)}) %all-reduce.12.cloned.1.call-update) | async-done | bytes 524304 | tf_op jit(solution)/shard_map/psum | solution.py:40
  143.7 2.1 fusion.4
  145.8 1.6 dynamic-slice_select_fusion.3
  147.6 0.7 broadcast_compare_fusion
  148.2 153.8 %all-reduce.16.cloned.1.call-done = (f32[2048,128]{1,0:T(8,128)}, f32[2048,128]{1,0:T(8,128)}, f32[256,128]{1,0:T(8,128)}, f32[256,128]{1,0:T(8,128)}) async-done(((f32[2048,128]{1,0:T(8,128)}, f32[2048,128]{1,0:T(8,128)}, f32[256,128]{1,0:T(8,128)}, f32[256,128]{1,0:T(8,128)}), (f32[2048,128]{1,0:T(8,128)}, f32[2048,128]{1,0:T(8,128)}, f32[256,128]{1,0:T(8,128)}, ...) | async-done | bytes 2359312 | tf_op jit(solution)/shard_map/psum | solution.py:60
  302.0 2.4 select_dynamic-update-slice_fusion.1
  304.4 2.4 fusion.27
  307.5 6.3 convolution_select_fusion.1
  313.8 112.8 %all-reduce.8.cloned.1.call-done = f32[128,128]{0,1:T(8,128)} async-done(((f32[128,128]{0,1:T(8,128)}), f32[128,128]{0,1:T(8,128)}) %all-reduce.8.cloned.1.call-update) | async-done | bytes 65552 | tf_op jit(solution)/shard_map/psum | solution.py:84
  426.6 0.9 copy.14
  427.6 0.9 fusion.22
  428.5 11.7 %cholesky.44 = f32[128,128]{1,0:T(8,128)S(1)} custom-call(f32[128,128]{1,0:T(8,128)S(1)} %fusion.22), custom_call_target="Cholesky" | custom-call | tf_op jit(solution)/shard_map/jit(cholesky)/cholesky | solution.py:85
  440.9 0.7 fusion.15
  441.5 9.8 %custom-call.10 = f32[1,128,128]{1,2,0:T(8,128)S(1)} custom-call(f32[1,128,128]{2,1,0:T(8,128)S(1)} %fusion.15), custom_call_target="InvertDiagBlocksLowerTriangular" | custom-call | tf_op jit(solution)/shard_map/triangular_solve/custom-call.0 | solution.py:27
  451.3 1.1 convolution_bitcast_fusion.2
  452.4 1.0 copy-done.5
  453.4 5.3 fusion.28
  460.0 41.8 %all-gather.5.cloned.1.call-done = f32[2048,512]{1,0:T(8,128)} async-done(((f32[128,512]{1,0:T(8,128)}), f32[2048,512]{1,0:T(8,128)}) %all-gather.5.cloned.1.call-update) | async-done | bytes 4194320 | tf_op jit(solution)/shard_map/all_gather | solution.py:8
  501.9 2.6 reduce_sum.38
  504.5 5.6 subtract_select_fusion.1
  511.3 1.1 fusion.5
  512.3 3.0 fusion.6
  515.4 0.7 dynamic-slice_select_fusion.2
  516.0 1.1 dynamic-slice_select_fusion
  517.4 153.0 %all-reduce.14.cloned.1.call-done = (f32[2048,128]{1,0:T(8,128)}, f32[2048,128]{1,0:T(8,128)}, f32[256,128]{1,0:T(8,128)}, f32[256,128]{1,0:T(8,128)}) async-done(((f32[2048,128]{1,0:T(8,128)}, f32[2048,128]{1,0:T(8,128)}, f32[256,128]{1,0:T(8,128)}, f32[256,128]{1,0:T(8,128)}), (f32[2048,128]{1,0:T(8,128)}, f32[2048,128]{1,0:T(8,128)}, f32[256,128]{1,0:T(8,128)}, ...) | async-done | bytes 2359312 | tf_op jit(solution)/shard_map/psum | solution.py:60
  670.4 2.4 select_dynamic-update-slice_fusion
  672.8 2.4 fusion.29
  675.5 6.3 convolution_select_fusion
  681.9 113.1 %all-reduce.10.cloned.1.call-done = f32[128,128]{0,1:T(8,128)} async-done(((f32[128,128]{0,1:T(8,128)}), f32[128,128]{0,1:T(8,128)}) %all-reduce.10.cloned.1.call-update) | async-done | bytes 65552 | tf_op jit(solution)/shard_map/psum | solution.py:84
  795.0 0.9 copy.16
  795.9 0.9 fusion.19
  796.8 11.7 %cholesky.55 = f32[128,128]{1,0:T(8,128)S(1)} custom-call(f32[128,128]{1,0:T(8,128)S(1)} %fusion.19), custom_call_target="Cholesky" | custom-call | tf_op jit(solution)/shard_map/jit(cholesky)/cholesky | solution.py:85
  809.2 0.7 fusion.16
  809.9 9.8 %custom-call.11 = f32[1,128,128]{1,2,0:T(8,128)S(1)} custom-call(f32[1,128,128]{2,1,0:T(8,128)S(1)} %fusion.16), custom_call_target="InvertDiagBlocksLowerTriangular" | custom-call | tf_op jit(solution)/shard_map/triangular_solve/custom-call.0 | solution.py:27
  819.7 1.1 convolution_bitcast_fusion.1
  820.8 1.0 copy-done.7
  821.7 5.3 fusion.30
  827.1 1.4 compare_or_fusion
  828.8 41.4 %all-gather.7.cloned.1.call-done = f32[2048,512]{1,0:T(8,128)} async-done(((f32[128,512]{1,0:T(8,128)}), f32[2048,512]{1,0:T(8,128)}) %all-gather.7.cloned.1.call-update) | async-done | bytes 4194320 | tf_op jit(solution)/shard_map/all_gather | solution.py:8
  870.2 2.9 reduce_sum.39
  873.2 6.8 subtract_select_fusion
  879.9 0.8 pad_maximum_fusion
  881.4 1.2 fusion.3
  (66 shorter events, 6.0 us)
Async XLA Ops:
  7.2 4.4 copy-start
  7.2 136.5 %all-reduce.12.cloned.1.call-start = ((), (), s32[]{:S(2)}) async-start(), calls=%async_computation.2 | async-start | bytes 1048576 | tf_op jit(solution)/shard_map/psum | solution.py:40
  9.6 2.0 copy-start.1
  11.6 4.6 copy-start.18
  11.6 8.2 copy-start.19
  16.1 286.0 %all-reduce.16.cloned.1.call-start = ((), (), s32[]{:S(2)}) async-start(), calls=%async_computation.6 | async-start | bytes 4718592 | tf_op jit(solution)/shard_map/psum | solution.py:60
  147.4 279.2 %all-reduce.8.cloned.1.call-start = ((), (), s32[]{:S(2)}) async-start(), calls=%async_computation | async-start | bytes 131072 | tf_op jit(solution)/shard_map/psum | solution.py:84
  302.0 2.4 copy-start.3
  306.9 195.0 %all-gather.5.cloned.1.call-start = ((), (), s32[]{:S(2)}) async-start(), calls=%async_computation.3 | async-start | bytes 4456448 | tf_op jit(solution)/shard_map/all_gather | solution.py:8
  427.6 32.1 %copy-start.14 = (f32[256,128]{1,0:T(8,128)S(1)}, f32[256,128]{1,0:T(8,128)}, u32[]{:S(2)}) copy-start(f32[256,128]{1,0:T(8,128)} %get-tuple-element.12) | copy-start | bytes 393220
  452.4 1.0 copy-start.5
  458.7 45.8 %copy-start.6 = (f32[2048,128]{0,1:T(8,128)S(1)}, f32[2048,128]{0,1:T(8,128)}, u32[]{:S(2)}) copy-start(f32[2048,128]{0,1:T(8,128)} %copy-done.5) | copy-start | bytes 3145732
  458.7 211.6 %all-reduce.14.cloned.1.call-start = ((), (), s32[]{:S(2)}) async-start(), calls=%async_computation.5 | async-start | bytes 4718592 | tf_op jit(solution)/shard_map/psum | solution.py:60
  504.5 5.6 copy-start.11
  504.5 6.3 copy-start.13
  504.5 6.3 copy-start.16
  510.1 5.9 copy-start.2
  511.2 4.1 copy-start.9
  517.2 277.8 %all-reduce.10.cloned.1.call-start = ((), (), s32[]{:S(2)}) async-start(), calls=%async_computation.1 | async-start | bytes 131072 | tf_op jit(solution)/shard_map/psum | solution.py:84
  670.4 2.4 copy-start.4
  675.3 195.0 %all-gather.7.cloned.1.call-start = ((), (), s32[]{:S(2)}) async-start(), calls=%async_computation.4 | async-start | bytes 4456448 | tf_op jit(solution)/shard_map/all_gather | solution.py:8
  795.9 32.5 %copy-start.15 = (f32[256,128]{1,0:T(8,128)S(1)}, f32[256,128]{1,0:T(8,128)}, u32[]{:S(2)}) copy-start(f32[256,128]{1,0:T(8,128)} %get-tuple-element.8) | copy-start | bytes 393220
  820.8 1.0 copy-start.7
  827.1 46.1 %copy-start.8 = (f32[2048,128]{0,1:T(8,128)S(1)}, f32[2048,128]{0,1:T(8,128)}, u32[]{:S(2)}) copy-start(f32[2048,128]{0,1:T(8,128)} %copy-done.7) | copy-start | bytes 3145732
  873.2 6.8 copy-start.12
  873.2 8.2 copy-start.10
  873.2 8.2 copy-start.17
Sparse Core Ops, SparseCore 0:
  16.2 127.4 all-reduce.11
  147.5 154.4 all-reduce.15
  307.0 119.5 all-reduce.7
  458.9 42.9 all-gather.4
  517.3 153.0 all-reduce.13
  675.4 119.5 all-reduce.9
  827.2 42.9 all-gather.6
